TPU v7x, 32 devices: a whole 2x2x4 slice. The times are simulated.
32 devices in a mesh: dp: 16 (over z, y, core), tensor: 2 (over x).
Axes of the slice: x: 2, y: 2, z: 4, core: 2. Of those that a mesh axis runs over, the one named last changes fastest.
Arguments:
- tokens: bfloat16 [4096, 1024], P(('dp', 'tensor')), may hold values from -6 to 6
- out_cotangent: bfloat16 [4096, 1024], P(('dp', 'tensor')), may hold values from -6 to 6
- seq_lengths: int32 [16], P('dp'), may hold values from 1 to 256, 2048 in all
- norm_gain1: float32 [1024], replicated, may hold values from 0.1 to 1.9
- query_weight: bfloat16 [1024, 1024], P('dp', 'tensor'), may hold values from -0.1875 to 0.1875
- key_weight: bfloat16 [1024, 1024], P('dp', 'tensor'), may hold values from -0.1875 to 0.1875
- value_weight: bfloat16 [1024, 2048], P('dp', 'tensor'), may hold values from -0.1875 to 0.1875
- out_gate_weight: bfloat16 [1024, 2048], P('dp', 'tensor'), may hold values from -0.1875 to 0.1875
- beta_weight: bfloat16 [1024, 8], P('dp', 'tensor'), may hold values from -0.1875 to 0.1875
- decay_weight: bfloat16 [1024, 8], P('dp', 'tensor'), may hold values from -0.1875 to 0.1875
- conv_query: float32 [4, 1024], P(None, 'tensor'), may hold values from -3 to 3
- conv_key: float32 [4, 1024], P(None, 'tensor'), may hold values from -3 to 3
- conv_value: float32 [4, 2048], P(None, 'tensor'), may hold values from -3 to 3
- decay_log_rate: float32 [8], P('tensor'), may hold values from -4 to 1
- decay_bias: float32 [8], P('tensor'), may hold values from -4 to 0
- out_gain: float32 [256], replicated, may hold values from 0.1 to 1.9
- out_weight: bfloat16 [1024, 2048], P('dp', 'tensor'), may hold values from -0.25 to 0.25
- norm_gain2: float32 [1024], replicated, may hold values from 0.1 to 1.9
- ffn_gate_weight: bfloat16 [1024, 2816], P('dp', 'tensor'), may hold values from -0.1875 to 0.1875
- ffn_up_weight: bfloat16 [1024, 2816], P('dp', 'tensor'), may hold values from -0.1875 to 0.1875
- ffn_down_weight: bfloat16 [1024, 2816], P('dp', 'tensor'), may hold values from -0.109375 to 0.109375
Outputs:
- output: bfloat16 [4096, 1024], P(('dp', 'tensor'))
- grad_tokens: bfloat16 [4096, 1024], P(('dp', 'tensor'))
- grad_norm_gain1: float32 [1024], replicated
- grad_query_weight: float32 [1024, 1024], P('dp', 'tensor')
- grad_key_weight: float32 [1024, 1024], P('dp', 'tensor')
- grad_value_weight: float32 [1024, 2048], P('dp', 'tensor')
- grad_out_gate_weight: float32 [1024, 2048], P('dp', 'tensor')
- grad_beta_weight: float32 [1024, 8], P('dp', 'tensor')
- grad_decay_weight: float32 [1024, 8], P('dp', 'tensor')
- grad_conv_query: float32 [4, 1024], replicated
- grad_conv_key: float32 [4, 1024], replicated
- grad_conv_value: float32 [4, 2048], replicated
- grad_decay_log_rate: float32 [8], replicated
- grad_decay_bias: float32 [8], replicated
- grad_out_gain: float32 [256], replicated
- grad_out_weight: float32 [1024, 2048], P('dp', 'tensor')
- grad_norm_gain2: float32 [1024], replicated
- grad_ffn_gate_weight: float32 [1024, 2816], P('dp', 'tensor')
- grad_ffn_up_weight: float32 [1024, 2816], P('dp', 'tensor')
- grad_ffn_down_weight: float32 [1024, 2816], P('dp', 'tensor')
Inputs may be any that keep to these rules, and one draw needn't show every extreme that they name: `seq_lengths`: the number of valid tokens of each sequence; the largest is exactly 256.
All inputs are finite; a program needn't handle non-finite values. No bound on the sum of `seq_lengths` on one device may be relied on, other than what follows from the above.
Results may differ from a plain program's by a relative error of at most 0.012.
Values may be sent and summed in bfloat16 or wider, within the bound.
No kernel may reach another device: no remote copies, remote signals or barrier semaphores. Data moves between devices by JAX's collectives and lax.ppermute only.
A program may use at most 192 MiB of HBM per device.

v0:
```python
import jax
import jax.numpy as jnp
from jax import lax
from jax.sharding import PartitionSpec as P

GROUP = 64
highest = lax.Precision.HIGHEST


def plain_dot(left, right):
    return jnp.dot(left, right, preferred_element_type=jnp.float32)


def left_dot(left, right):
    return lax.dot_general(
        left, right, (((0,), (0,)), ((), ())), preferred_element_type=jnp.float32
    )


def right_dot(left, right):
    return lax.dot_general(
        left, right, (((1,), (1,)), ((), ())), preferred_element_type=jnp.float32
    )


def exact_dot(left, right):
    return jnp.dot(left, right, precision=highest)


def rms_rows(inputs, gain):
    wide_rows = inputs.astype(jnp.float32)
    inverse = lax.rsqrt(jnp.mean(wide_rows * wide_rows, -1, keepdims=True) + 1e-05)
    normed = wide_rows * inverse
    return (normed, inverse, (normed * gain).astype(jnp.bfloat16))


def rms_back(grad_rows, normed, inverse, gain):
    scaled = grad_rows * gain
    grad_in = inverse * (scaled - normed * jnp.mean(scaled * normed, -1, keepdims=True))
    return (grad_in, jnp.sum(grad_rows * normed, 0))


def causal_conv(projected, kernel):
    kernel_len = kernel.shape[0]
    summed = kernel[kernel_len - 1] * projected
    for offset in range(1, kernel_len):
        shifted = jnp.pad(projected[:-offset], ((offset, 0), (0, 0)))
        summed = summed + kernel[kernel_len - 1 - offset] * shifted
    return summed


def delta_block(state, element):
    block_query, block_key, block_value, block_beta, block_gate = element
    block_len = block_key.shape[0]
    value_dim = block_value.shape[1]
    lower_all = jnp.tril(jnp.ones((block_len, block_len), dtype=bool))
    strict_lower = jnp.tril(jnp.ones((block_len, block_len), dtype=bool), -1)
    cumulative = jnp.cumsum(block_gate)
    spread = cumulative[:, None] - cumulative[None, :]
    decays = jnp.where(lower_all, jnp.exp(jnp.where(lower_all, spread, 0.0)), 0.0)
    key_key = exact_dot(block_key, block_key.T)
    coupling = jnp.where(strict_lower, block_beta[:, None] * key_key * decays, 0.0)
    stacked = jnp.concatenate(
        [
            block_beta[:, None] * block_value,
            (block_beta * jnp.exp(cumulative))[:, None] * block_key,
        ],
        axis=1,
    )
    solved = lax.linalg.triangular_solve(
        coupling + jnp.eye(block_len, dtype=jnp.float32),
        stacked,
        left_side=True,
        lower=True,
        unit_diagonal=True,
    )
    updates = solved[:, :value_dim] - exact_dot(solved[:, value_dim:], state.T)
    query_key = jnp.where(lower_all, exact_dot(block_query, block_key.T) * decays, 0.0)
    outputs = jnp.exp(cumulative)[:, None] * exact_dot(block_query, state.T) + exact_dot(
        query_key, updates
    )
    final_log = cumulative[-1]
    new_state = jnp.exp(final_log) * state + exact_dot(
        updates.T, block_key * jnp.exp(final_log - cumulative)[:, None]
    )
    return (new_state, outputs)


def delta_rule(query_rows, key_rows, value_rows, beta_rows, log_gates, block_len):
    length, head_count, key_dim = key_rows.shape
    value_dim = value_rows.shape[2]
    blocks = length // block_len

    def split_heads(array):
        shaped = array.reshape((blocks, block_len) + array.shape[1:])
        return jnp.moveaxis(shaped, 2, 0)

    def one_head(head_query, head_key, head_value, head_beta, head_gate):
        start_state = jnp.zeros((value_dim, key_dim), jnp.float32)
        unused, outputs = lax.scan(
            delta_block, start_state, (head_query, head_key, head_value, head_beta, head_gate)
        )
        return outputs

    per_head = jax.vmap(one_head)(
        split_heads(query_rows),
        split_heads(key_rows),
        split_heads(value_rows),
        split_heads(beta_rows),
        split_heads(log_gates),
    )
    return jnp.transpose(per_head, (1, 2, 0, 3)).reshape(length, head_count, value_dim)


def mixer(
    proj_query,
    proj_key,
    proj_value,
    proj_gate,
    proj_beta,
    proj_decay,
    conv_query,
    conv_key,
    conv_value,
    decay_log_rate,
    decay_bias,
    out_gain,
):
    length = proj_query.shape[0]
    head_count = proj_beta.shape[1]
    query_rows = jax.nn.silu(causal_conv(proj_query, conv_query)).reshape(length, head_count, -1)
    key_rows = jax.nn.silu(causal_conv(proj_key, conv_key)).reshape(length, head_count, -1)
    value_rows = jax.nn.silu(causal_conv(proj_value, conv_value)).reshape(length, head_count, -1)
    key_dim = query_rows.shape[2]
    query_rows = (
        query_rows
        * lax.rsqrt(jnp.sum(query_rows * query_rows, -1, keepdims=True) + 1e-06)
        * key_dim ** (-0.5)
    )
    key_rows = key_rows * lax.rsqrt(jnp.sum(key_rows * key_rows, -1, keepdims=True) + 1e-06)
    beta_rows = jax.nn.sigmoid(proj_beta)
    log_gates = -jnp.exp(decay_log_rate) * jax.nn.softplus(proj_decay + decay_bias)
    mixed = delta_rule(query_rows, key_rows, value_rows, beta_rows, log_gates, GROUP)
    inverse = lax.rsqrt(jnp.mean(mixed * mixed, -1, keepdims=True) + 1e-05)
    gated = mixed * inverse * out_gain * jax.nn.silu(proj_gate.reshape(length, head_count, -1))
    return gated.reshape(length, -1)


def split_columns(array, widths):
    pieces = []
    offset = 0
    for width in widths:
        pieces.append(array[:, offset : offset + width])
        offset = offset + width
    return pieces


def on_device(
    tokens,
    out_cotangent,
    seq_lengths,
    norm_gain1,
    query_weight,
    key_weight,
    value_weight,
    out_gate_weight,
    beta_weight,
    decay_weight,
    conv_query,
    conv_key,
    conv_value,
    decay_log_rate,
    decay_bias,
    out_gain,
    out_weight,
    norm_gain2,
    ffn_gate_weight,
    ffn_up_weight,
    ffn_down_weight,
):
    local_rows = tokens.shape[0]
    tensor_index = lax.axis_index("tensor")
    tensor_count = lax.axis_size("tensor")
    seq_length = seq_lengths[0]
    local_pos = tensor_index * local_rows + jnp.arange(local_rows, dtype=jnp.int32)
    local_mask = (local_pos < seq_length).astype(jnp.float32)[:, None]
    whole_mask = (jnp.arange(local_rows * tensor_count, dtype=jnp.int32) < seq_length).astype(
        jnp.bfloat16
    )[:, None]
    key_cols = query_weight.shape[1]
    value_cols = value_weight.shape[1]
    head_cols = beta_weight.shape[1]
    hidden_cols = ffn_gate_weight.shape[1]
    mixer_widths = [key_cols, key_cols, value_cols, value_cols, head_cols, head_cols]
    mixer_joined = jnp.concatenate(
        [query_weight, key_weight, value_weight, out_gate_weight, beta_weight, decay_weight], axis=1
    )
    ffn_joined = jnp.concatenate([ffn_gate_weight, ffn_up_weight], axis=1)
    normed1, inverse1, hidden1 = rms_rows(tokens, norm_gain1)
    whole1 = lax.all_gather(hidden1, "tensor", axis=0, tiled=True)
    mixer_full = (
        lax.all_gather(mixer_joined, "dp", axis=0, tiled=True),
        lax.all_gather(out_weight, "dp", axis=0, tiled=True),
    )
    projections = split_columns(plain_dot(whole1, mixer_full[0]), mixer_widths)
    mixed_out, pullback = jax.vjp(
        mixer,
        projections[0],
        projections[1],
        projections[2],
        projections[3],
        projections[4],
        projections[5],
        conv_query,
        conv_key,
        conv_value,
        decay_log_rate,
        decay_bias,
        out_gain,
    )
    mixed_half = mixed_out.astype(jnp.bfloat16)
    out_full = mixer_full[1]
    branch = lax.psum_scatter(
        right_dot(mixed_half, out_full), "tensor", scatter_dimension=0, tiled=True
    )
    residual = tokens.astype(jnp.float32) + branch
    normed2, inverse2, hidden2 = rms_rows(residual, norm_gain2)
    whole2 = lax.all_gather(hidden2, "tensor", axis=0, tiled=True)
    ffn_full = (
        lax.all_gather(ffn_joined, "dp", axis=0, tiled=True),
        lax.all_gather(ffn_down_weight, "dp", axis=0, tiled=True),
    )
    pre_both = plain_dot(whole2, ffn_full[0])
    gate_pre = pre_both[:, :hidden_cols]
    up_pre = pre_both[:, hidden_cols:]
    gate_act = jax.nn.silu(gate_pre)
    inner_act = (gate_act * up_pre).astype(jnp.bfloat16)
    down_full = ffn_full[1]
    ffn_branch = lax.psum_scatter(
        right_dot(inner_act, down_full).astype(jnp.bfloat16),
        "tensor",
        scatter_dimension=0,
        tiled=True,
    ).astype(jnp.float32)
    output = (local_mask * (residual + ffn_branch)).astype(jnp.bfloat16)
    grad_whole = lax.all_gather(out_cotangent, "tensor", axis=0, tiled=True) * whole_mask
    grad_inner = plain_dot(grad_whole, ffn_full[1])
    sigma_gate = jax.nn.sigmoid(gate_pre)
    grad_gate_pre = (
        grad_inner * up_pre * sigma_gate * (1.0 + gate_pre * (1.0 - sigma_gate))
    ).astype(jnp.bfloat16)
    grad_up_pre = (grad_inner * gate_act).astype(jnp.bfloat16)
    grad_pre_both = jnp.concatenate([grad_gate_pre, grad_up_pre], axis=1)
    grad_hidden2 = lax.psum_scatter(
        right_dot(grad_pre_both, ffn_full[0]), "tensor", scatter_dimension=0, tiled=True
    )
    grad_normed2, second_gain_gradient = rms_back(grad_hidden2, normed2, inverse2, norm_gain2)
    grad_residual = local_mask * out_cotangent.astype(jnp.float32) + grad_normed2
    gate_up_part = left_dot(whole2, grad_pre_both)
    down_part = left_dot(grad_whole, inner_act)
    ffn_shard = lax.psum_scatter(
        jnp.concatenate([gate_up_part, down_part], axis=1), "dp", scatter_dimension=0, tiled=True
    )
    grad_whole1 = lax.all_gather(grad_residual.astype(jnp.bfloat16), "tensor", axis=0, tiled=True)
    grad_mixed = plain_dot(grad_whole1, mixer_full[1])
    mixer_gradient_list = pullback(grad_mixed)
    grad_projs = jnp.concatenate(
        [member.astype(jnp.bfloat16) for member in mixer_gradient_list[:6]], axis=1
    )
    grad_hidden1 = lax.psum_scatter(
        right_dot(grad_projs, mixer_full[0]).astype(jnp.bfloat16),
        "tensor",
        scatter_dimension=0,
        tiled=True,
    ).astype(jnp.float32)
    grad_normed1, first_gain_gradient = rms_back(grad_hidden1, normed1, inverse1, norm_gain1)
    grad_tokens = (grad_residual + grad_normed1).astype(jnp.bfloat16)
    proj_part = left_dot(whole1, grad_projs)
    out_part = left_dot(grad_whole1, mixed_half)
    mixer_shard = lax.psum_scatter(
        jnp.concatenate([proj_part, out_part], axis=1), "dp", scatter_dimension=0, tiled=True
    )
    mixer_grads = split_columns(mixer_shard, mixer_widths + [value_cols])
    ffn_grads = split_columns(ffn_shard, [hidden_cols, hidden_cols, hidden_cols])

    def widen(element, axis_pos):
        size_one = element.shape[axis_pos]
        shape_all = list(element.shape)
        shape_all[axis_pos] = size_one * tensor_count
        return lax.dynamic_update_slice_in_dim(
            jnp.zeros(shape_all, jnp.float32), element, tensor_index * size_one, axis_pos
        )

    small_sums = lax.psum(
        (
            first_gain_gradient,
            second_gain_gradient,
            mixer_gradient_list[11],
            widen(mixer_gradient_list[6], 1),
            widen(mixer_gradient_list[7], 1),
            widen(mixer_gradient_list[8], 1),
            widen(mixer_gradient_list[9], 0),
            widen(mixer_gradient_list[10], 0),
        ),
        ("dp", "tensor"),
    )
    return (
        output,
        grad_tokens,
        small_sums[0],
        mixer_grads[0],
        mixer_grads[1],
        mixer_grads[2],
        mixer_grads[3],
        mixer_grads[4],
        mixer_grads[5],
        small_sums[3],
        small_sums[4],
        small_sums[5],
        small_sums[6],
        small_sums[7],
        small_sums[2],
        mixer_grads[6],
        small_sums[1],
        ffn_grads[0],
        ffn_grads[1],
        ffn_grads[2],
    )


def solution(mesh):
    in_specs = (
        P(("dp", "tensor"), None),
        P(("dp", "tensor"), None),
        P("dp"),
        P(),
        P("dp", "tensor"),
        P("dp", "tensor"),
        P("dp", "tensor"),
        P("dp", "tensor"),
        P("dp", "tensor"),
        P("dp", "tensor"),
        P(None, "tensor"),
        P(None, "tensor"),
        P(None, "tensor"),
        P("tensor"),
        P("tensor"),
        P(),
        P("dp", "tensor"),
        P(),
        P("dp", "tensor"),
        P("dp", "tensor"),
        P("dp", "tensor"),
    )
    out_specs = (
        P(("dp", "tensor"), None),
        P(("dp", "tensor"), None),
        P(),
        P("dp", "tensor"),
        P("dp", "tensor"),
        P("dp", "tensor"),
        P("dp", "tensor"),
        P("dp", "tensor"),
        P("dp", "tensor"),
        P(),
        P(),
        P(),
        P(),
        P(),
        P(),
        P("dp", "tensor"),
        P(),
        P("dp", "tensor"),
        P("dp", "tensor"),
        P("dp", "tensor"),
    )
    return jax.shard_map(
        on_device, mesh=mesh, in_specs=in_specs, out_specs=out_specs, check_vma=False
    )
```

profile of v0, /device:TPU:8, one launch (start us, length us, event | category | flops | bytes accessed | tf_op | source)
XLA Modules:
  0.0 1243.3 jit_solution(5438580144339664088)
XLA Ops:
  14.0 8.7 all_gather.24
  23.0 52.0 %all-gather.5.cloned.1.call-done = bf16[1024,3080]{1,0:T(8,128)(2,1)} async-done(((bf16[64,3080]{1,0:T(8,128)(2,1)}), bf16[1024,3080]{1,0:T(8,128)(2,1)}) %all-gather.5.cloned.1.call-update) | async-done | bytes 6307856 | tf_op jit(solution)/shard_map/all_gather | solution.py:202
  75.0 5.6 fusion.229
  109.3 144.0 %while.98 = (s32[]{:T(128)}, f32[4,256,128]{2,1,0:T(8,128)S(1)}, f32[4,4,64,256]{3,1,2,0:T(4,128)}, f32[4,4,64,64]{3,2,1,0:T(8,128)}, f32[4,4,128,64]{2,3,1,0:T(...) while((s32[]{:T(128)}, f32[4,256,128]{2,1,0:T(8,128)S(1)}, ...), condition=%wide.region_5.6_spmd.clone.clone, body=%wide.region_3.5_spmd.clone.clone.sunk | while | flops 479990848 | bytes 12846126 | solution.py:100
  114.7 19.7 %custom-call.48 = f32[4,1,64,64]{2,3,1,0:T(8,128)S(1)} custom-call(f32[4,1,64,64]{3,2,1,0:T(8,128)S(1)} %add_bitcast_fusion.4), custom_call_target="InvertDiagBlocksLowerTriangular" | custom-call | tf_op jit(solution)/shard_map/jvp(vmap())/while/body/eval_jaxpr/triangular_solve | solution.py:70
  150.6 19.7 %custom-call.48 = f32[4,1,64,64]{2,3,1,0:T(8,128)S(1)} custom-call(f32[4,1,64,64]{3,2,1,0:T(8,128)S(1)} %add_bitcast_fusion.4), custom_call_target="InvertDiagBlocksLowerTriangular" | custom-call | tf_op jit(solution)/shard_map/jvp(vmap())/while/body/eval_jaxpr/triangular_solve | solution.py:70
  186.6 19.7 %custom-call.48 = f32[4,1,64,64]{2,3,1,0:T(8,128)S(1)} custom-call(f32[4,1,64,64]{3,2,1,0:T(8,128)S(1)} %add_bitcast_fusion.4), custom_call_target="InvertDiagBlocksLowerTriangular" | custom-call | tf_op jit(solution)/shard_map/jvp(vmap())/while/body/eval_jaxpr/triangular_solve | solution.py:70
  222.5 19.7 %custom-call.48 = f32[4,1,64,64]{2,3,1,0:T(8,128)S(1)} custom-call(f32[4,1,64,64]{3,2,1,0:T(8,128)S(1)} %add_bitcast_fusion.4), custom_call_target="InvertDiagBlocksLowerTriangular" | custom-call | tf_op jit(solution)/shard_map/jvp(vmap())/while/body/eval_jaxpr/triangular_solve | solution.py:70
  267.8 14.3 %all_gather.30 = bf16[256,1024]{1,0:T(8,128)(2,1)S(1)} all-gather(bf16[128,1024]{1,0:T(8,128)(2,1)S(1)} %copy-done.41), channel_id=1, replica_groups=mesh['dp'=16,'tensor'=2] {'tensor'}, dimensions={0}, use_global_device_ids=true | all-gather | bytes 786432 | tf_op jit(solution)/shard_map/all_gather | solution.py:246
  282.1 7.2 reduce-scatter.9.cloned.1.call-done
  290.7 8.8 all_gather.27
  299.5 50.0 %all-gather.9.cloned.1.call-done = bf16[1024,2816]{1,0:T(8,128)(2,1)} async-done(((bf16[64,2816]{1,0:T(8,128)(2,1)}), bf16[1024,2816]{1,0:T(8,128)(2,1)}) %all-gather.9.cloned.1.call-update) | async-done | bytes 5767184 | tf_op jit(solution)/shard_map/all_gather | solution.py:230
  349.5 5.9 fusion.231
  355.4 38.8 %all-gather.11.cloned.1.call-done = bf16[1024,1408]{1,0:T(8,128)(2,1)} async-done(((bf16[64,1408]{1,0:T(8,128)(2,1)}), bf16[1024,1408]{1,0:T(8,128)(2,1)}) %all-gather.11.cloned.1.call-update) | async-done | bytes 2883600 | tf_op jit(solution)/shard_map/all_gather | solution.py:231
  394.3 5.0 multiply_convert_fusion.1
  415.9 4.8 fusion.191
  420.8 5.9 fusion.169
  428.6 10.6 reduce-scatter.11.cloned.1.call-done
  441.7 8.9 all_gather.31
  464.9 191.4 %while.99 = (s32[]{:T(128)}, f32[4,256,128]{2,1,0:T(8,128)S(1)}, f32[4,4,64,128]{3,2,1,0:T(8,128)}, f32[4,4,64,128]{3,2,1,0:T(8,128)}, f32[4,4,64,256]{3,2,1,0:T...) while((s32[]{:T(128)}, f32[4,256,128]{2,1,0:T(8,128)S(1)}, ...), condition=%wide.region_24.25_spmd.clone.clone, body=%wide.region_13.24_spmd.clone.clone.sunk | while | flops 971683904 | bytes 18991880 | solution.py:100
  472.6 19.7 %custom-call.49 = f32[4,1,64,64]{2,3,1,0:T(8,128)S(1)} custom-call(f32[4,1,64,64]{3,2,1,0:T(8,128)S(1)} %add_bitcast_fusion.5), custom_call_target="InvertDiagBlocksLowerTriangular" | custom-call | tf_op jit(solution)/shard_map/transpose(jvp(vmap()))/while/body/eval_jaxpr/triangular_solve | solution.py:70
  520.4 19.7 %custom-call.49 = f32[4,1,64,64]{2,3,1,0:T(8,128)S(1)} custom-call(f32[4,1,64,64]{3,2,1,0:T(8,128)S(1)} %add_bitcast_fusion.5), custom_call_target="InvertDiagBlocksLowerTriangular" | custom-call | tf_op jit(solution)/shard_map/transpose(jvp(vmap()))/while/body/eval_jaxpr/triangular_solve | solution.py:70
  568.2 19.7 %custom-call.49 = f32[4,1,64,64]{2,3,1,0:T(8,128)S(1)} custom-call(f32[4,1,64,64]{3,2,1,0:T(8,128)S(1)} %add_bitcast_fusion.5), custom_call_target="InvertDiagBlocksLowerTriangular" | custom-call | tf_op jit(solution)/shard_map/transpose(jvp(vmap()))/while/body/eval_jaxpr/triangular_solve | solution.py:70
  616.0 19.7 %custom-call.49 = f32[4,1,64,64]{2,3,1,0:T(8,128)S(1)} custom-call(f32[4,1,64,64]{3,2,1,0:T(8,128)S(1)} %add_bitcast_fusion.5), custom_call_target="InvertDiagBlocksLowerTriangular" | custom-call | tf_op jit(solution)/shard_map/transpose(jvp(vmap()))/while/body/eval_jaxpr/triangular_solve | solution.py:70
  682.8 4.9 multiply_reduce_fusion.3
  701.1 5.6 convolution_convert_fusion
  706.8 11.9 pad_maximum_fusion
  722.5 7.2 pad_maximum_fusion.1
  729.6 19.0 %copy.246 = f32[1024,4104]{1,0:T(8,128)} copy(f32[1024,4104]{0,1:T(8,128)} %pad_maximum_fusion.1) | data formatting | bytes 33619968
  753.3 153.3 %reduce-scatter.17.cloned.1.call-done = f32[64,4224]{1,0:T(8,128)} async-done(((f32[1024,4224]{1,0:T(8,128)}), f32[64,4224]{1,0:T(8,128)}) %reduce-scatter.17.cloned.1.call-update) | async-done | bytes 1081360 | tf_op jit(solution)/shard_map/reduce_scatter | solution.py:261
  908.8 182.9 %reduce-scatter.19.cloned.1.call-done = f32[64,4104]{1,0:T(8,128)} async-done(((f32[1024,4104]{1,0:T(8,128)}), f32[64,4104]{1,0:T(8,128)}) %reduce-scatter.19.cloned.1.call-update) | async-done | bytes 1050640
  1097.7 128.7 %all-reduce.36.cloned.1.call-done = (f32[1024]{0:T(1024)}, f32[4,1024]{1,0:T(4,128)}, f32[4,1024]{1,0:T(4,128)}, f32[4,2048]{1,0:T(4,128)}, f32[8]{0:T(128)}, /*index=5*/f32[8]{0:T(128)}, f32[256]{0:T(256)}, f32[1024]{0:T(1024)}) async-done(((f32[1024]{0:T(1024)}, f32[4,1024]{1,0:T(4,128)}, f32[4,1024]{1,0:T(4,128)}, f32[4,2048]{1,0:T(4,128)}, f32[8]{0:T(128)}, /*index=5*/f32[8]{0:T(128)}, f32[256]{0:T(256)}, ...) | async-done | bytes 74832 | tf_op jit(solution)/shard_map/psum | solution.py:294
  (703 shorter events, 328.1 us)
Async XLA Ops:
  7.2 67.7 %all-gather.5.cloned.1.call-start = ((), (), s32[]{:S(2)}) async-start(), calls=%async_computation.6 | async-start | bytes 6963200 | tf_op jit(solution)/shard_map/all_gather | solution.py:202
  10.8 251.2 %all-gather.7.cloned.1.call-start = ((), (), s32[]{:S(2)}) async-start(), calls=%async_computation.7 | async-start | bytes 2228224 | tf_op jit(solution)/shard_map/all_gather | solution.py:203
  11.5 277.8 %reduce-scatter.9.cloned.1.call-start = ((), (), s32[]{:S(2)}) async-start(), calls=%async_computation.8 | async-start | bytes 1572864 | tf_op jit(solution)/shard_map/reduce_scatter | solution.py:223
  12.9 67.7 %copy-start.105 = (f32[128]{0:T(128)}, f32[128]{0:T(128)S(1)}, u32[]{:S(2)}) copy-start(f32[128]{0:T(128)S(1)} %add_rsqrt_fusion.3) | copy-start | bytes 1540
  22.7 52.3 %copy-start.31 = (bf16[256,1024]{1,0:T(8,128)(2,1)}, bf16[256,1024]{1,0:T(8,128)(2,1)S(1)}, u32[]{:S(2)}) copy-start(bf16[256,1024]{1,0:T(8,128)(2,1)S(1)} %all_gather.24) | copy-start | bytes 1572868
  22.7 236.4 %copy-start.67 = (f32[1,2,4,128]{3,1,2,0:T(2,128)}, f32[1,2,4,128]{3,1,2,0:T(2,128)S(1)}, u32[]{:S(2)}) copy-start(f32[1,2,4,128]{3,1,2,0:T(2,128)S(1)} %copy.322) | copy-start | bytes 12292
  22.7 62.8 %copy-start.111 = (f32[4]{0:T(128)}, f32[4]{0:T(128)S(1)}, u32[]{:S(2)}) copy-start(f32[4]{0:T(128)S(1)} %exponential_negate_fusion) | copy-start | bytes 52
  22.8 63.0 %copy-start.85 = (f32[1,512]{1,0:T(1,128)}, f32[1,512]{1,0:T(1,128)S(1)}, u32[]{:S(2)}) copy-start(f32[1,512]{1,0:T(1,128)S(1)} %get-tuple-element.2632) | copy-start | bytes 6148
  22.8 63.0 %copy-start.89 = (f32[1,512]{1,0:T(1,128)}, f32[1,512]{1,0:T(1,128)S(1)}, u32[]{:S(2)}) copy-start(f32[1,512]{1,0:T(1,128)S(1)} %get-tuple-element.2633) | copy-start | bytes 6148
  22.8 63.0 %copy-start.93 = (f32[1,512]{1,0:T(1,128)}, f32[1,512]{1,0:T(1,128)S(1)}, u32[]{:S(2)}) copy-start(f32[1,512]{1,0:T(1,128)S(1)} %get-tuple-element.2631) | copy-start | bytes 6148
  22.8 63.0 %copy-start.97 = (f32[1,512]{1,0:T(1,128)}, f32[1,512]{1,0:T(1,128)S(1)}, u32[]{:S(2)}) copy-start(f32[1,512]{1,0:T(1,128)S(1)} %get-tuple-element.2630) | copy-start | bytes 6148
  22.8 63.0 %copy-start.83 = (f32[1,512]{1,0:T(1,128)}, f32[1,512]{1,0:T(1,128)S(1)}, u32[]{:S(2)}) copy-start(f32[1,512]{1,0:T(1,128)S(1)} %get-tuple-element.2636) | copy-start | bytes 6148
  22.8 63.0 %copy-start.87 = (f32[1,512]{1,0:T(1,128)}, f32[1,512]{1,0:T(1,128)S(1)}, u32[]{:S(2)}) copy-start(f32[1,512]{1,0:T(1,128)S(1)} %get-tuple-element.2637) | copy-start | bytes 6148
  22.8 63.0 %copy-start.91 = (f32[1,512]{1,0:T(1,128)}, f32[1,512]{1,0:T(1,128)S(1)}, u32[]{:S(2)}) copy-start(f32[1,512]{1,0:T(1,128)S(1)} %get-tuple-element.2635) | copy-start | bytes 6148
  22.9 63.0 %copy-start.95 = (f32[1,512]{1,0:T(1,128)}, f32[1,512]{1,0:T(1,128)S(1)}, u32[]{:S(2)}) copy-start(f32[1,512]{1,0:T(1,128)S(1)} %get-tuple-element.2634) | copy-start | bytes 6148
  22.9 72.0 %copy-start.69 = (f32[1,1024]{1,0:T(1,128)}, f32[1,1024]{1,0:T(1,128)S(1)}, u32[]{:S(2)}) copy-start(f32[1,1024]{1,0:T(1,128)S(1)} %get-tuple-element.2628) | copy-start | bytes 12292
  22.9 72.0 %copy-start.71 = (f32[1,1024]{1,0:T(1,128)}, f32[1,1024]{1,0:T(1,128)S(1)}, u32[]{:S(2)}) copy-start(f32[1,1024]{1,0:T(1,128)S(1)} %get-tuple-element.2629) | copy-start | bytes 12292
  22.9 72.0 %copy-start.73 = (f32[1,1024]{1,0:T(1,128)}, f32[1,1024]{1,0:T(1,128)S(1)}, u32[]{:S(2)}) copy-start(f32[1,1024]{1,0:T(1,128)S(1)} %get-tuple-element.2627) | copy-start | bytes 12292
  22.9 72.0 %copy-start.81 = (f32[1,1024]{1,0:T(1,128)}, f32[1,1024]{1,0:T(1,128)S(1)}, u32[]{:S(2)}) copy-start(f32[1,1024]{1,0:T(1,128)S(1)} %get-tuple-element.2626) | copy-start | bytes 12292
  265.6 25.0 %copy-start.62 = (f32[1024]{0:T(1024)S(1)}, f32[1024]{0:T(1024)}, u32[]{:S(2)}) copy-start(f32[1024]{0:T(1024)} %param.42) | copy-start | bytes 12292
  265.6 83.9 %all-gather.9.cloned.1.call-start = ((), (), s32[]{:S(2)}) async-start(), calls=%async_computation.9 | async-start | bytes 6127616 | tf_op jit(solution)/shard_map/all_gather | solution.py:230
  266.5 127.8 %all-gather.11.cloned.1.call-start = ((), (), s32[]{:S(2)}) async-start(), calls=%async_computation.10 | async-start | bytes 3063808 | tf_op jit(solution)/shard_map/all_gather | solution.py:231
  267.0 159.7 %reduce-scatter.13.cloned.1.call-start = ((), (), s32[]{:S(2)}) async-start(), calls=%async_computation.12 | async-start | bytes 1572864 | tf_op jit(solution)/shard_map/reduce_scatter | solution.py:254
  267.8 126.5 %copy-start.113 = (bf16[256]{0:T(256)(128)(2,1)}, bf16[256]{0:T(256)(128)(2,1)S(1)}, u32[]{:S(2)}) copy-start(bf16[256]{0:T(256)(128)(2,1)S(1)} %compare_convert_fusion) | copy-start | bytes 1540
  282.1 112.1 %copy-start.29 = (bf16[256,1024]{1,0:T(8,128)(2,1)}, bf16[256,1024]{1,0:T(8,128)(2,1)S(1)}, u32[]{:S(2)}) copy-start(bf16[256,1024]{1,0:T(8,128)(2,1)S(1)} %all_gather.30) | copy-start | bytes 1572868
  290.6 64.8 %copy-start.107 = (f32[128]{0:T(128)}, f32[128]{0:T(128)S(1)}, u32[]{:S(2)}) copy-start(f32[128]{0:T(128)S(1)} %add_rsqrt_fusion.2) | copy-start | bytes 1540
  299.5 55.9 %copy-start.33 = (bf16[256,1024]{1,0:T(8,128)(2,1)}, bf16[256,1024]{1,0:T(8,128)(2,1)S(1)}, u32[]{:S(2)}) copy-start(bf16[256,1024]{1,0:T(8,128)(2,1)S(1)} %all_gather.27) | copy-start | bytes 1572868
  403.2 36.1 %reduce-scatter.11.cloned.1.call-start = ((), (), s32[]{:S(2)}) async-start(), calls=%async_computation.11 | async-start | bytes 786432 | tf_op jit(solution)/shard_map/reduce_scatter | solution.py:239
  415.8 333.5 %reduce-scatter.15.cloned.1.call-start = ((), (), s32[]{:S(2)}) async-start(), calls=%async_computation.13 | async-start | bytes 786432 | tf_op jit(solution)/shard_map/reduce_scatter | solution.py:270
  706.7 199.9 %reduce-scatter.17.cloned.1.call-start = ((), (), s32[]{:S(2)}) async-start(), calls=%async_computation.14 | async-start | bytes 18382848 | tf_op jit(solution)/shard_map/reduce_scatter | solution.py:261
  718.8 373.0 %reduce-scatter.19.cloned.1.call-start = ((), (), s32[]{:S(2)}) async-start(), calls=%async_computation.15 | async-start | bytes 18382848
  748.6 477.7 %all-reduce.36.cloned.1.call-start = ((), (), s32[]{:S(2)}) async-start(), calls=%async_computation.16 | async-start | bytes 151552 | tf_op jit(solution)/shard_map/psum | solution.py:294
  (102 other events, 509.5 us)
Sparse Core Ops, SparseCore 0:
  10.9 64.0 all-gather.4
  77.1 39.0 all-gather.6
  265.7 23.5 reduce-scatter.8
  292.1 57.4 all-gather.8
  351.6 42.5 all-gather.10
  403.3 18.9 reduce-scatter.12
  424.6 14.6 reduce-scatter.10
  706.9 14.6 reduce-scatter.14
  725.6 180.9 reduce-scatter.16
  910.6 181.0 reduce-scatter.18
  1099.9 126.4 all-reduce.35
where the time goes:
time: 1250 us; the launch traced here: 1240 us
  waiting for transfers between devices  625 us (50%)
  other arithmetic  276 us (22%)
  matrix products  149 us (12%)
  local copies, waits for them, and re-layouts  134 us (11%)
  blocking collectives  40.8 us (3%)
  between operations  16.3 us (1%)
    unnamed x12, waiting for transfers between devices  184 us
    another operation x40, other arithmetic, delta_block(): lax.linalg.triangular_solve(coupling + jnp.eye(block_len, dtype=jnp.float...  162 us
    reduce_scatter x1, waiting for transfers between devices, on_device(): lax.psum_scatter(jnp.concatenate([gate_up_part, down_part], axis=1), 'dp'...  153 us
    psum x1, waiting for transfers between devices, on_device(): lax.psum((first_gain_gradient, second_gain_gradient, mixer_gradient_list[...  129 us
    dot_general x72, matrix products, exact_dot(): return jnp.dot(left, right, precision=highest)  82 us
    all_gather x1, waiting for transfers between devices, on_device(): lax.all_gather(mixer_joined, 'dp', axis=0, tiled=True)  52 us
    all_gather x1, waiting for transfers between devices, on_device(): lax.all_gather(ffn_joined, 'dp', axis=0, tiled=True)  50 us
    unnamed x256, local copies, waits for them, and re-layouts  41.7 us
  transfers between devices with their start and end apart: 11, of which 8 were waited for; matrix products, arithmetic and copies ran while one was open for 22% of the time, Pallas kernels for 0%

commit v1 on v0

--- a/solution.py
+++ b/solution.py
@@ -292,17 +292,20 @@
         )
 
     small_sums = lax.psum(
-        (
-            first_gain_gradient,
-            second_gain_gradient,
-            mixer_gradient_list[11],
-            widen(mixer_gradient_list[6], 1),
-            widen(mixer_gradient_list[7], 1),
-            widen(mixer_gradient_list[8], 1),
-            widen(mixer_gradient_list[9], 0),
-            widen(mixer_gradient_list[10], 0),
+        lax.psum(
+            (
+                first_gain_gradient,
+                second_gain_gradient,
+                mixer_gradient_list[11],
+                widen(mixer_gradient_list[6], 1),
+                widen(mixer_gradient_list[7], 1),
+                widen(mixer_gradient_list[8], 1),
+                widen(mixer_gradient_list[9], 0),
+                widen(mixer_gradient_list[10], 0),
+            ),
+            "tensor",
         ),
-        ("dp", "tensor"),
+        "dp",
     )
     return (
         output,

time: 1250 us -> 1240 us (level)
  waiting for transfers between devices: 625 us -> 612 us
    psum x1, waiting for transfers between devices: 129 us -> 0.01 us  [on_device(): lax.psum((first_gain_gradient, second_gain_gradient, mixer_gradient_list[...]
    psum x0 -> x1, waiting for transfers between devices: none -> 89 us  [on_device(): lax.psum(lax.psum((first_gain_gradient, second_gain_gradient, mixer_gradi...]
    reduce_scatter x1, waiting for transfers between devices: 153 us -> 166 us  [on_device(): lax.psum_scatter(jnp.concatenate([gate_up_part, down_part], axis=1), 'dp'...]
    unnamed x12 -> x13, waiting for transfers between devices: 184 us -> 184 us
    unnamed x256 -> x254, local copies, waits for them, and re-layouts: 41.7 us -> 41.7 us
  transfers between devices with their start and end apart: 11 -> 12, of which waited for: 8 -> 10; matrix products, arithmetic and copies ran while one was open for 22% -> 22% of each run, Pallas kernels for 0% -> 0%
where the time goes in v1:
time: 1240 us; the launch traced here: 1230 us
  waiting for transfers between devices  612 us (49%)
  other arithmetic  276 us (22%)
  matrix products  150 us (12%)
  local copies, waits for them, and re-layouts  134 us (11%)
  blocking collectives  40.2 us (3%)
  between operations  16.6 us (1%)
    unnamed x13, waiting for transfers between devices  184 us
    reduce_scatter x1, waiting for transfers between devices, on_device(): lax.psum_scatter(jnp.concatenate([gate_up_part, down_part], axis=1), 'dp'...  166 us
    another operation x40, other arithmetic, delta_block(): lax.linalg.triangular_solve(coupling + jnp.eye(block_len, dtype=jnp.float...  162 us
    psum x1, waiting for transfers between devices, on_device(): lax.psum(lax.psum((first_gain_gradient, second_gain_gradient, mixer_gradi...  89 us
    dot_general x72, matrix products, exact_dot(): return jnp.dot(left, right, precision=highest)  82.1 us
    all_gather x1, waiting for transfers between devices, on_device(): lax.all_gather(mixer_joined, 'dp', axis=0, tiled=True)  52 us
    all_gather x1, waiting for transfers between devices, on_device(): lax.all_gather(ffn_joined, 'dp', axis=0, tiled=True)  50.1 us
    unnamed x254, local copies, waits for them, and re-layouts  41.7 us
  transfers between devices with their start and end apart: 12, of which 10 were waited for; matrix products, arithmetic and copies ran while one was open for 22% of the time, Pallas kernels for 0%

profile of v1, /device:TPU:8, one launch (start us, length us, event | category | flops | bytes accessed | tf_op | source)
XLA Modules:
  0.0 1230.3 jit_solution(15022270990851615085)
XLA Ops:
  14.0 8.7 all_gather.24
  23.0 52.0 %all-gather.5.cloned.1.call-done = bf16[1024,3080]{1,0:T(8,128)(2,1)} async-done(((bf16[64,3080]{1,0:T(8,128)(2,1)}), bf16[1024,3080]{1,0:T(8,128)(2,1)}) %all-gather.5.cloned.1.call-update) | async-done | bytes 6307856 | tf_op jit(solution)/shard_map/all_gather | solution.py:202
  75.0 5.6 fusion.229
  109.9 144.1 %while.98 = (s32[]{:T(128)}, f32[4,256,128]{2,1,0:T(8,128)S(1)}, f32[4,4,64,256]{3,1,2,0:T(4,128)}, f32[4,4,64,64]{3,2,1,0:T(8,128)}, f32[4,4,128,64]{2,3,1,0:T(...) while((s32[]{:T(128)}, f32[4,256,128]{2,1,0:T(8,128)S(1)}, ...), condition=%wide.region_5.6_spmd.clone.clone, body=%wide.region_3.5_spmd.clone.clone.sunk | while | flops 479990848 | bytes 12846126 | solution.py:100
  115.2 19.7 %custom-call.48 = f32[4,1,64,64]{2,3,1,0:T(8,128)S(1)} custom-call(f32[4,1,64,64]{3,2,1,0:T(8,128)S(1)} %add_bitcast_fusion.4), custom_call_target="InvertDiagBlocksLowerTriangular" | custom-call | tf_op jit(solution)/shard_map/jvp(vmap())/while/body/eval_jaxpr/triangular_solve | solution.py:70
  151.2 19.7 %custom-call.48 = f32[4,1,64,64]{2,3,1,0:T(8,128)S(1)} custom-call(f32[4,1,64,64]{3,2,1,0:T(8,128)S(1)} %add_bitcast_fusion.4), custom_call_target="InvertDiagBlocksLowerTriangular" | custom-call | tf_op jit(solution)/shard_map/jvp(vmap())/while/body/eval_jaxpr/triangular_solve | solution.py:70
  187.2 19.7 %custom-call.48 = f32[4,1,64,64]{2,3,1,0:T(8,128)S(1)} custom-call(f32[4,1,64,64]{3,2,1,0:T(8,128)S(1)} %add_bitcast_fusion.4), custom_call_target="InvertDiagBlocksLowerTriangular" | custom-call | tf_op jit(solution)/shard_map/jvp(vmap())/while/body/eval_jaxpr/triangular_solve | solution.py:70
  223.2 19.7 %custom-call.48 = f32[4,1,64,64]{2,3,1,0:T(8,128)S(1)} custom-call(f32[4,1,64,64]{3,2,1,0:T(8,128)S(1)} %add_bitcast_fusion.4), custom_call_target="InvertDiagBlocksLowerTriangular" | custom-call | tf_op jit(solution)/shard_map/jvp(vmap())/while/body/eval_jaxpr/triangular_solve | solution.py:70
  268.4 14.1 %all_gather.30 = bf16[256,1024]{1,0:T(8,128)(2,1)S(1)} all-gather(bf16[128,1024]{1,0:T(8,128)(2,1)S(1)} %copy-done.41), channel_id=1, replica_groups=mesh['dp'=16,'tensor'=2] {'tensor'}, dimensions={0}, use_global_device_ids=true | all-gather | bytes 786432 | tf_op jit(solution)/shard_map/all_gather | solution.py:246
  282.5 7.5 reduce-scatter.9.cloned.1.call-done
  291.3 8.8 all_gather.27
  300.2 50.1 %all-gather.9.cloned.1.call-done = bf16[1024,2816]{1,0:T(8,128)(2,1)} async-done(((bf16[64,2816]{1,0:T(8,128)(2,1)}), bf16[1024,2816]{1,0:T(8,128)(2,1)}) %all-gather.9.cloned.1.call-update) | async-done | bytes 5767184 | tf_op jit(solution)/shard_map/all_gather | solution.py:230
  350.3 5.9 fusion.231
  356.1 38.9 %all-gather.11.cloned.1.call-done = bf16[1024,1408]{1,0:T(8,128)(2,1)} async-done(((bf16[64,1408]{1,0:T(8,128)(2,1)}), bf16[1024,1408]{1,0:T(8,128)(2,1)}) %all-gather.11.cloned.1.call-update) | async-done | bytes 2883600 | tf_op jit(solution)/shard_map/all_gather | solution.py:231
  395.0 5.0 multiply_convert_fusion.1
  416.5 4.9 fusion.191
  424.9 15.0 %reduce-scatter.11.cloned.1.call-done = bf16[128,1024]{1,0:T(8,128)(2,1)} async-done(((bf16[256,1024]{1,0:T(8,128)(2,1)}), bf16[128,1024]{1,0:T(8,128)(2,1)}) %reduce-scatter.11.cloned.1.call-update) | async-done | bytes 262160 | tf_op jit(solution)/shard_map/reduce_scatter | solution.py:239
  442.3 8.5 all_gather.31
  465.3 191.6 %while.99 = (s32[]{:T(128)}, f32[4,256,128]{2,1,0:T(8,128)S(1)}, f32[4,4,64,128]{3,2,1,0:T(8,128)}, f32[4,4,64,128]{3,2,1,0:T(8,128)}, f32[4,4,64,256]{3,2,1,0:T...) while((s32[]{:T(128)}, f32[4,256,128]{2,1,0:T(8,128)S(1)}, ...), condition=%wide.region_24.25_spmd.clone.clone, body=%wide.region_13.24_spmd.clone.clone.sunk | while | flops 971683904 | bytes 18991880 | solution.py:100
  473.0 19.7 %custom-call.49 = f32[4,1,64,64]{2,3,1,0:T(8,128)S(1)} custom-call(f32[4,1,64,64]{3,2,1,0:T(8,128)S(1)} %add_bitcast_fusion.5), custom_call_target="InvertDiagBlocksLowerTriangular" | custom-call | tf_op jit(solution)/shard_map/transpose(jvp(vmap()))/while/body/eval_jaxpr/triangular_solve | solution.py:70
  520.8 19.7 %custom-call.49 = f32[4,1,64,64]{2,3,1,0:T(8,128)S(1)} custom-call(f32[4,1,64,64]{3,2,1,0:T(8,128)S(1)} %add_bitcast_fusion.5), custom_call_target="InvertDiagBlocksLowerTriangular" | custom-call | tf_op jit(solution)/shard_map/transpose(jvp(vmap()))/while/body/eval_jaxpr/triangular_solve | solution.py:70
  568.6 19.7 %custom-call.49 = f32[4,1,64,64]{2,3,1,0:T(8,128)S(1)} custom-call(f32[4,1,64,64]{3,2,1,0:T(8,128)S(1)} %add_bitcast_fusion.5), custom_call_target="InvertDiagBlocksLowerTriangular" | custom-call | tf_op jit(solution)/shard_map/transpose(jvp(vmap()))/while/body/eval_jaxpr/triangular_solve | solution.py:70
  616.4 19.7 %custom-call.49 = f32[4,1,64,64]{2,3,1,0:T(8,128)S(1)} custom-call(f32[4,1,64,64]{3,2,1,0:T(8,128)S(1)} %add_bitcast_fusion.5), custom_call_target="InvertDiagBlocksLowerTriangular" | custom-call | tf_op jit(solution)/shard_map/transpose(jvp(vmap()))/while/body/eval_jaxpr/triangular_solve | solution.py:70
  701.6 5.7 convolution_convert_fusion
  707.6 7.1 fusion.169
  715.2 6.9 reduce-scatter.15.cloned.1.call-done
  724.1 11.7 pad_maximum_fusion
  739.5 7.2 pad_maximum_fusion.1
  746.7 18.0 %copy.246 = f32[1024,4104]{1,0:T(8,128)} copy(f32[1024,4104]{0,1:T(8,128)} %pad_maximum_fusion.1) | data formatting | bytes 33619968
  766.9 166.2 %reduce-scatter.17.cloned.1.call-done = f32[64,4224]{1,0:T(8,128)} async-done(((f32[1024,4224]{1,0:T(8,128)}), f32[64,4224]{1,0:T(8,128)}) %reduce-scatter.17.cloned.1.call-update) | async-done | bytes 1081360 | tf_op jit(solution)/shard_map/reduce_scatter | solution.py:261
  935.3 183.0 %reduce-scatter.19.cloned.1.call-done = f32[64,4104]{1,0:T(8,128)} async-done(((f32[1024,4104]{1,0:T(8,128)}), f32[64,4104]{1,0:T(8,128)}) %reduce-scatter.19.cloned.1.call-update) | async-done | bytes 1050640
  1124.3 89.0 %all-reduce.38.cloned.1.call-done = (f32[1024]{0:T(1024)}, f32[4,1024]{1,0:T(4,128)}, f32[4,1024]{1,0:T(4,128)}, f32[4,2048]{1,0:T(4,128)}, f32[8]{0:T(128)}, /*index=5*/f32[8]{0:T(128)}, f32[256]{0:T(256)}, f32[1024]{0:T(1024)}) async-done(((f32[1024]{0:T(1024)}, f32[4,1024]{1,0:T(4,128)}, f32[4,1024]{1,0:T(4,128)}, f32[4,2048]{1,0:T(4,128)}, f32[8]{0:T(128)}, /*index=5*/f32[8]{0:T(128)}, f32[256]{0:T(256)}, ...) | async-done | bytes 74832 | tf_op jit(solution)/shard_map/psum | solution.py:294
  (704 shorter events, 335.2 us)
Async XLA Ops:
  7.2 67.8 %all-gather.5.cloned.1.call-start = ((), (), s32[]{:S(2)}) async-start(), calls=%async_computation.6 | async-start | bytes 6963200 | tf_op jit(solution)/shard_map/all_gather | solution.py:202
  10.8 251.8 %all-gather.7.cloned.1.call-start = ((), (), s32[]{:S(2)}) async-start(), calls=%async_computation.7 | async-start | bytes 2228224 | tf_op jit(solution)/shard_map/all_gather | solution.py:203
  11.5 278.4 %reduce-scatter.9.cloned.1.call-start = ((), (), s32[]{:S(2)}) async-start(), calls=%async_computation.8 | async-start | bytes 1572864 | tf_op jit(solution)/shard_map/reduce_scatter | solution.py:223
  12.9 67.7 %copy-start.104 = (f32[128]{0:T(128)}, f32[128]{0:T(128)S(1)}, u32[]{:S(2)}) copy-start(f32[128]{0:T(128)S(1)} %add_rsqrt_fusion.3) | copy-start | bytes 1540
  22.7 52.3 %copy-start.30 = (bf16[256,1024]{1,0:T(8,128)(2,1)}, bf16[256,1024]{1,0:T(8,128)(2,1)S(1)}, u32[]{:S(2)}) copy-start(bf16[256,1024]{1,0:T(8,128)(2,1)S(1)} %all_gather.24) | copy-start | bytes 1572868
  22.7 237.0 %copy-start.66 = (f32[1,2,4,128]{3,1,2,0:T(2,128)}, f32[1,2,4,128]{3,1,2,0:T(2,128)S(1)}, u32[]{:S(2)}) copy-start(f32[1,2,4,128]{3,1,2,0:T(2,128)S(1)} %copy.322) | copy-start | bytes 12292
  22.7 62.9 %copy-start.110 = (f32[4]{0:T(128)}, f32[4]{0:T(128)S(1)}, u32[]{:S(2)}) copy-start(f32[4]{0:T(128)S(1)} %exponential_negate_fusion) | copy-start | bytes 52
  22.8 63.1 %copy-start.84 = (f32[1,512]{1,0:T(1,128)}, f32[1,512]{1,0:T(1,128)S(1)}, u32[]{:S(2)}) copy-start(f32[1,512]{1,0:T(1,128)S(1)} %get-tuple-element.2640) | copy-start | bytes 6148
  22.8 63.1 %copy-start.88 = (f32[1,512]{1,0:T(1,128)}, f32[1,512]{1,0:T(1,128)S(1)}, u32[]{:S(2)}) copy-start(f32[1,512]{1,0:T(1,128)S(1)} %get-tuple-element.2641) | copy-start | bytes 6148
  22.8 63.1 %copy-start.92 = (f32[1,512]{1,0:T(1,128)}, f32[1,512]{1,0:T(1,128)S(1)}, u32[]{:S(2)}) copy-start(f32[1,512]{1,0:T(1,128)S(1)} %get-tuple-element.2639) | copy-start | bytes 6148
  22.8 63.1 %copy-start.96 = (f32[1,512]{1,0:T(1,128)}, f32[1,512]{1,0:T(1,128)S(1)}, u32[]{:S(2)}) copy-start(f32[1,512]{1,0:T(1,128)S(1)} %get-tuple-element.2638) | copy-start | bytes 6148
  22.8 63.1 %copy-start.82 = (f32[1,512]{1,0:T(1,128)}, f32[1,512]{1,0:T(1,128)S(1)}, u32[]{:S(2)}) copy-start(f32[1,512]{1,0:T(1,128)S(1)} %get-tuple-element.2644) | copy-start | bytes 6148
  22.9 63.1 %copy-start.86 = (f32[1,512]{1,0:T(1,128)}, f32[1,512]{1,0:T(1,128)S(1)}, u32[]{:S(2)}) copy-start(f32[1,512]{1,0:T(1,128)S(1)} %get-tuple-element.2645) | copy-start | bytes 6148
  22.9 63.1 %copy-start.90 = (f32[1,512]{1,0:T(1,128)}, f32[1,512]{1,0:T(1,128)S(1)}, u32[]{:S(2)}) copy-start(f32[1,512]{1,0:T(1,128)S(1)} %get-tuple-element.2643) | copy-start | bytes 6148
  22.9 63.1 %copy-start.94 = (f32[1,512]{1,0:T(1,128)}, f32[1,512]{1,0:T(1,128)S(1)}, u32[]{:S(2)}) copy-start(f32[1,512]{1,0:T(1,128)S(1)} %get-tuple-element.2642) | copy-start | bytes 6148
  22.9 72.6 %copy-start.68 = (f32[1,1024]{1,0:T(1,128)}, f32[1,1024]{1,0:T(1,128)S(1)}, u32[]{:S(2)}) copy-start(f32[1,1024]{1,0:T(1,128)S(1)} %get-tuple-element.2636) | copy-start | bytes 12292
  22.9 72.6 %copy-start.70 = (f32[1,1024]{1,0:T(1,128)}, f32[1,1024]{1,0:T(1,128)S(1)}, u32[]{:S(2)}) copy-start(f32[1,1024]{1,0:T(1,128)S(1)} %get-tuple-element.2637) | copy-start | bytes 12292
  22.9 72.6 %copy-start.72 = (f32[1,1024]{1,0:T(1,128)}, f32[1,1024]{1,0:T(1,128)S(1)}, u32[]{:S(2)}) copy-start(f32[1,1024]{1,0:T(1,128)S(1)} %get-tuple-element.2635) | copy-start | bytes 12292
  22.9 72.6 %copy-start.80 = (f32[1,1024]{1,0:T(1,128)}, f32[1,1024]{1,0:T(1,128)S(1)}, u32[]{:S(2)}) copy-start(f32[1,1024]{1,0:T(1,128)S(1)} %get-tuple-element.2634) | copy-start | bytes 12292
  266.2 84.0 %all-gather.9.cloned.1.call-start = ((), (), s32[]{:S(2)}) async-start(), calls=%async_computation.9 | async-start | bytes 6127616 | tf_op jit(solution)/shard_map/all_gather | solution.py:230
  267.1 127.9 %all-gather.11.cloned.1.call-start = ((), (), s32[]{:S(2)}) async-start(), calls=%async_computation.10 | async-start | bytes 3063808 | tf_op jit(solution)/shard_map/all_gather | solution.py:231
  267.7 155.3 %reduce-scatter.13.cloned.1.call-start = ((), (), s32[]{:S(2)}) async-start(), calls=%async_computation.12 | async-start | bytes 1572864 | tf_op jit(solution)/shard_map/reduce_scatter | solution.py:254
  268.4 126.6 %copy-start.112 = (bf16[256]{0:T(256)(128)(2,1)}, bf16[256]{0:T(256)(128)(2,1)S(1)}, u32[]{:S(2)}) copy-start(bf16[256]{0:T(256)(128)(2,1)S(1)} %compare_convert_fusion) | copy-start | bytes 1540
  282.5 112.5 %copy-start.29 = (bf16[256,1024]{1,0:T(8,128)(2,1)}, bf16[256,1024]{1,0:T(8,128)(2,1)S(1)}, u32[]{:S(2)}) copy-start(bf16[256,1024]{1,0:T(8,128)(2,1)S(1)} %all_gather.30) | copy-start | bytes 1572868
  291.2 64.9 %copy-start.106 = (f32[128]{0:T(128)}, f32[128]{0:T(128)S(1)}, u32[]{:S(2)}) copy-start(f32[128]{0:T(128)S(1)} %add_rsqrt_fusion.2) | copy-start | bytes 1540
  300.2 56.0 %copy-start.32 = (bf16[256,1024]{1,0:T(8,128)(2,1)}, bf16[256,1024]{1,0:T(8,128)(2,1)S(1)}, u32[]{:S(2)}) copy-start(bf16[256,1024]{1,0:T(8,128)(2,1)S(1)} %all_gather.27) | copy-start | bytes 1572868
  403.8 36.1 %reduce-scatter.11.cloned.1.call-start = ((), (), s32[]{:S(2)}) async-start(), calls=%async_computation.11 | async-start | bytes 786432 | tf_op jit(solution)/shard_map/reduce_scatter | solution.py:239
  407.8 314.4 %reduce-scatter.15.cloned.1.call-start = ((), (), s32[]{:S(2)}) async-start(), calls=%async_computation.13 | async-start | bytes 786432 | tf_op jit(solution)/shard_map/reduce_scatter | solution.py:270
  707.4 59.4 %all-reduce.40.cloned.1.call-start = ((), (), s32[]{:S(2)}) async-start(), calls=%async_computation.17 | async-start | bytes 151552 | tf_op jit(solution)/shard_map/psum | solution.py:295
  724.0 209.0 %reduce-scatter.17.cloned.1.call-start = ((), (), s32[]{:S(2)}) async-start(), calls=%async_computation.14 | async-start | bytes 18382848 | tf_op jit(solution)/shard_map/reduce_scatter | solution.py:261
  735.8 382.5 %reduce-scatter.19.cloned.1.call-start = ((), (), s32[]{:S(2)}) async-start(), calls=%async_computation.15 | async-start | bytes 18382848
  764.7 448.5 %all-reduce.38.cloned.1.call-start = ((), (), s32[]{:S(2)}) async-start(), calls=%async_computation.16 | async-start | bytes 151552 | tf_op jit(solution)/shard_map/psum | solution.py:294
  (102 other events, 610.1 us)
Sparse Core Ops, SparseCore 0:
  10.9 64.0 all-gather.4
  77.2 39.0 all-gather.6
  266.3 23.5 reduce-scatter.8
  292.7 57.5 all-gather.8
  352.4 42.5 all-gather.10
  403.9 18.9 reduce-scatter.12
  425.2 14.6 reduce-scatter.10
  707.5 14.6 reduce-scatter.14
  726.5 21.5 all-reduce.39
  752.1 180.9 reduce-scatter.16
  937.2 181.0 reduce-scatter.18
  1122.6 90.5 all-reduce.37
